TPU v7x, 32 devices: a whole 2x2x4 slice. The times are simulated.
32 devices in a mesh: rep: 2 (over y), ep: 8 (over z, x), tp: 2 (over core).
Axes of the slice: x: 2, y: 2, z: 4, core: 2. Of those that a mesh axis runs over, the one named last changes fastest.
Arguments:
- resid: bfloat16 [1024, 1440], P(('rep', 'ep')), parts along dimension 0, may hold values from -6 to 6
- query: bfloat16 [1024, 2048], P(('rep', 'ep'), 'tp'), parts along dimension 0, may hold values from -400 to 400
- key_value_pages: bfloat16 [2, 12288, 16, 256], P(None, ('rep', 'ep'), None, 'tp'), parts along dimension 1, may hold values from -4 to 4
- page_table: int32 [1024, 12], P(('rep', 'ep')), parts along dimension 0, may hold values from 0 to 767, as said below
- ctx_len: int32 [1024], P(('rep', 'ep')), parts along dimension 0, may hold values from 2 to 192, as said below
- experts_chosen: int32 [1024, 4], P(('rep', 'ep')), parts along dimension 0, may hold values from 0 to 7, as said below
- router_logits: float32 [1024, 4], P(('rep', 'ep')), parts along dimension 0, may hold values from -25 to 300
- norm_gain: float32 [1440], replicated, may hold values from 0.25 to 1.75
- out_proj: bfloat16 [2048, 1440], P('tp'), may hold values from -0.125 to 0.125
- w_gate: bfloat16 [8, 1440, 1440], P('ep', None, 'tp'), may hold values from -0.15625 to 0.15625
- w_up: bfloat16 [8, 1440, 1440], P('ep', None, 'tp'), may hold values from -0.15625 to 0.15625
- w_down: bfloat16 [8, 1440, 1440], P('ep', 'tp'), may hold values from -3 to 3
Outputs:
- mixed: bfloat16 [1024, 1440], P(('rep', 'ep'), 'tp'), parts along dimension 0
There are 2 independent parts, one for each index of `rep`. A program takes and returns all parts, laid end to end along the dimension named above; an argument that names none is the same for every part. Nothing has to cross between parts.
Inputs may be any that keep to these rules, and one draw needn't show every extreme that they name: Each block of 64 tokens holds its own pool: the rows of page_table of one block together name each of its 768 pages once. `ctx_len`: every block of 64 tokens has a token with 192 positions. `experts_chosen`: each row names 4 different experts. Within the rows of one device no expert is named by more than 64 rows, and one expert is named by exactly 64 of them.
All inputs are finite; a program needn't handle non-finite values.
Results may differ from a plain program's by a relative error of at most 0.008.
Values may be sent and summed in bfloat16 or wider, within the bound.
No kernel may reach another device: no remote copies, remote signals or barrier semaphores. Data moves between devices by JAX's collectives and lax.ppermute only.
A program may use at most 128 MiB of HBM per device.

v0:
```python
import math
import jax
import jax.numpy as jnp
from jax import lax
from jax.sharding import PartitionSpec as P

HEAD_WIDTH = 64


def body(
    resid,
    query,
    key_value_pages,
    page_table,
    ctx_len,
    experts_chosen,
    router_logits,
    norm_gain,
    out_proj,
    w_gate,
    w_up,
    w_down,
):
    tok_rows = query.shape[0]
    model_width = resid.shape[1]
    query_heads = query.shape[1] // HEAD_WIDTH
    cache_heads = key_value_pages.shape[3] // HEAD_WIDTH
    group_width = query_heads // cache_heads
    positions = page_table.shape[1] * key_value_pages.shape[2]
    cached_keys = key_value_pages[0][page_table].reshape(
        tok_rows, positions, cache_heads, HEAD_WIDTH
    )
    cached_values = key_value_pages[1][page_table].reshape(
        tok_rows, positions, cache_heads, HEAD_WIDTH
    )
    query_block = query.reshape(tok_rows, cache_heads, group_width, HEAD_WIDTH)
    scores = jnp.einsum(
        "tgqd,tpgd->tgqp", query_block, cached_keys, preferred_element_type=jnp.float32
    ) * (1.0 / math.sqrt(HEAD_WIDTH))
    visible = jnp.arange(positions, dtype=jnp.int32)[None, :] < ctx_len[:, None]
    scores = jnp.where(visible[:, None, None, :], scores, -jnp.inf)
    row_max = jnp.max(scores, axis=3, keepdims=True)
    weights = jnp.exp(scores - row_max)
    probability = (weights / jnp.sum(weights, axis=3, keepdims=True)).astype(jnp.bfloat16)
    attended = jnp.einsum(
        "tgqp,tpgd->tgqd", probability, cached_values, preferred_element_type=jnp.float32
    )
    attended = attended.astype(jnp.bfloat16).reshape(tok_rows, query_heads * HEAD_WIDTH)
    head_part = jnp.dot(attended, out_proj, preferred_element_type=jnp.float32)
    half_cols = model_width // lax.axis_size("tp")
    offset = lax.axis_index("tp") * half_cols
    share = lax.psum_scatter(head_part, "tp", scatter_dimension=1, tiled=True)
    stream = lax.dynamic_slice_in_dim(resid, offset, half_cols, 1).astype(jnp.float32) + share
    mean_square = lax.psum(jnp.sum(stream * stream, axis=1), "tp") / model_width
    gain_cols = lax.dynamic_slice_in_dim(norm_gain, offset, half_cols, 0)
    normed = (stream * lax.rsqrt(mean_square + 1e-05)[:, None] * gain_cols).astype(jnp.bfloat16)
    gate_weights = jax.nn.softmax(router_logits, axis=1)
    top_count = experts_chosen.shape[1]
    local_experts = w_gate.shape[0]
    owners = lax.axis_size("ep")
    experts = local_experts * owners
    capacity = max(2, min(tok_rows, 2 * tok_rows * top_count // experts))
    chosen_flat = experts_chosen.reshape(-1)
    onehot = (chosen_flat[:, None] == jnp.arange(experts, dtype=jnp.int32)[None, :]).astype(
        jnp.int32
    )
    before = jnp.cumsum(onehot, axis=0, dtype=jnp.int32) - onehot
    slot_rank = jnp.sum(before * onehot, axis=1, dtype=jnp.int32)
    slot_index = (chosen_flat * capacity + slot_rank).reshape(tok_rows, top_count)
    slot_range = jnp.arange(experts * capacity, dtype=jnp.int32)
    placed = slot_index[:, :, None] == slot_range[None, None, :]
    dispatch = jnp.sum(placed.astype(jnp.float32), axis=1).astype(jnp.bfloat16)
    outgoing = lax.dot_general(
        dispatch, normed, (((0,), (0,)), ((), ())), preferred_element_type=jnp.float32
    )
    outgoing = outgoing.astype(jnp.bfloat16).reshape(
        owners, local_experts, capacity, normed.shape[1]
    )
    arrived_full = lax.all_gather(
        lax.all_to_all(outgoing, "ep", split_axis=0, concat_axis=0, tiled=True),
        "tp",
        axis=3,
        tiled=True,
    )
    gate_value = jnp.einsum(
        "sekd,edf->sekf", arrived_full, w_gate, preferred_element_type=jnp.float32
    )
    up_value = jnp.einsum("sekd,edf->sekf", arrived_full, w_up, preferred_element_type=jnp.float32)
    hidden = (gate_value * jax.nn.sigmoid(1.702 * gate_value) * (up_value + 1.0)).astype(
        jnp.bfloat16
    )
    partial_value = jnp.einsum("sekf,efd->sekd", hidden, w_down, preferred_element_type=jnp.float32)
    finished = lax.psum_scatter(partial_value, "tp", scatter_dimension=3, tiled=True).astype(
        jnp.bfloat16
    )
    returned = lax.all_to_all(finished, "ep", split_axis=0, concat_axis=0, tiled=True)
    combine = jnp.sum(placed.astype(jnp.float32) * gate_weights[:, :, None], axis=1)
    expert_mix = jnp.dot(
        combine,
        returned.reshape(experts * capacity, -1).astype(jnp.float32),
        precision=lax.Precision.HIGHEST,
    )
    mixed = stream + expert_mix
    return mixed.astype(jnp.bfloat16)


def solution(mesh):
    return jax.shard_map(
        body,
        mesh=mesh,
        in_specs=(
            P(("rep", "ep"), None),
            P(("rep", "ep"), "tp"),
            P(None, ("rep", "ep"), None, "tp"),
            P(("rep", "ep"), None),
            P(("rep", "ep")),
            P(("rep", "ep"), None),
            P(("rep", "ep"), None),
            P(),
            P("tp", None),
            P("ep", None, "tp"),
            P("ep", None, "tp"),
            P("ep", "tp", None),
        ),
        out_specs=P(("rep", "ep"), "tp"),
        check_vma=False,
    )
```

profile of v0, /device:TPU:0, one launch (start us, length us, event | category | flops | bytes accessed | tf_op | source)
XLA Modules:
  0.0 195.1 jit_solution(847633869631142299)
XLA Ops:
  6.5 0.0 copy-start
  6.5 0.0 copy-start.6
  6.5 0.0 reduce-scatter.7.cloned.1.call-start
  6.5 6.7 %slice_bitcast_fusion.1 = (bf16[768,16,128]{2,1,0:T(8,128)(2,1)}, bf16[768,16,128]{2,1,0:T(8,128)(2,1)}) fusion(bf16[2,768,16,128]{3,2,1,0:T(8,128)(2,1)} %param.14), kind=kLoop, calls=%fused_computation.9 | loop fusion | bytes 12582912 | tf_op jit(solution)/shard_map/squeeze | solution.py:30
  13.3 0.0 copy-done.6
  13.3 0.1 copy.53
  13.4 0.1 reshape.101
  13.5 4.9 %gather_fusion = bf16[768,16,128]{2,1,0:T(8,128)(2,1)} fusion(bf16[768,16,128]{2,1,0:T(8,128)(2,1)} %get-tuple-element.7, s32[1024]{0:T(1024)S(1)} %pad_clamp_fusion), kind=kCustom, calls=%fused_computation | custom fusion | bytes 6294528 | tf_op jit(solution)/shard_map/gather | solution.py:30
  18.3 0.0 copy-start.3
  18.3 11.7 %reshape.87 = bf16[64,192,2,64]{3,2,1,0:T(2,128)(2,1)} reshape(bf16[768,16,128]{2,1,0:T(8,128)(2,1)} %gather_fusion) | data formatting | bytes 6291456 | tf_op jit(solution)/shard_map/reshape | solution.py:30
  30.0 0.0 copy-done.3
  30.0 0.2 reshape.88
  30.2 0.0 copy-done.8
  30.2 0.1 iota_compare_fusion.1
  30.3 4.9 %gather_fusion.1 = bf16[768,16,128]{2,1,0:T(8,128)(2,1)} fusion(bf16[768,16,128]{2,1,0:T(8,128)(2,1)} %get-tuple-element.8, s32[1024]{0:T(1024)S(1)} %pad_clamp_fusion), kind=kCustom, calls=%fused_computation.1 | custom fusion | bytes 6294528 | tf_op jit(solution)/shard_map/gather | solution.py:33
  35.2 11.6 %reshape.89 = bf16[64,192,2,64]{3,2,1,0:T(2,128)(2,1)} reshape(bf16[768,16,128]{2,1,0:T(8,128)(2,1)} %gather_fusion.1) | data formatting | bytes 6291456 | tf_op jit(solution)/shard_map/reshape | solution.py:33
  46.8 7.3 %fusion.60 = (f32[64,2,8]{2,1,0:T(2,128)S(1)}, f32[64,2,8,192]{3,2,1,0:T(8,128)}) fusion(bf16[64,2,8,64]{3,2,1,0:T(8,128)(2,1)S(1)} %reshape.88, bf16[64,192,2,64]{3,2,1,0:T(2,128)(2,1)} %reshape.87, pred[64,192]{1,0:T(8,128)(4,1)S(1)} %iota_compare_fusion.1), kind=kOutput, calls=%fused_computation.69 | convolution fusion | flops 25952448 | bytes 4079616 | tf_op jit(solution)/shard_map/sub | solution.py:43
  54.1 4.9 %fusion.37 = bf16[64,2,8,64]{3,2,1,0:T(8,128)(2,1)S(1)} fusion(bf16[64,192,2,64]{3,2,1,0:T(2,128)(2,1)} %reshape.89, f32[64,2,8,192]{3,2,1,0:T(8,128)} %get-tuple-element.10, f32[64,2,8]{2,1,0:T(2,128)S(1)} %get-tuple-element.9), kind=kOutput, calls=%fused_computation.33 | convolution fusion | flops 25624576 | bytes 4067328 | tf_op jit(solution)/shard_map/tgqp,tpgd->tgqd/dot_general | solution.py:45
  59.0 0.2 reshape.90
  59.2 0.0 copy-done
  59.2 0.0 copy-start.5
  59.2 0.0 copy-start.7
  59.3 0.0 copy-start.4
  59.3 0.0 copy-start.2
  59.3 1.8 convolution_bitcast_fusion.1
  61.1 0.0 reduce-scatter.7.cloned.1.call-update
  61.1 0.2 all-gather.2.cloned.1.call-start
  61.3 0.0 copy-done.5
  61.3 0.1 copy.56
  61.4 0.1 eq.42
  61.5 0.1 eq.38
  61.7 0.6 reduce-window.6
  62.2 0.2 slice_reduce_fusion
  62.5 0.1 fusion.53
  62.6 0.1 reduce_sum.58
  62.7 0.1 copy.58
  62.8 0.0 copy-done.7
  62.8 0.1 dynamic_slice.7
  62.9 0.0 copy-done.4
  62.9 0.2 convert_reduce_fusion
  63.1 9.0 %reduce-scatter.7.cloned.1.call-done = f32[720,64]{1,0:T(8,128)} async-done(((f32[1440,64]{1,0:T(8,128)}), f32[720,64]{1,0:T(8,128)}) %reduce-scatter.7.cloned.1.call-update) | async-done | bytes 184336
  72.1 1.1 copy.65
  73.2 0.0 copy-done.2
  73.3 0.2 multiply_reduce_fusion
  73.5 2.5 %psum.7 = f32[64]{0:T(128)S(1)} all-reduce(f32[64]{0:T(128)S(1)} %multiply_reduce_fusion), channel_id=1, replica_groups=mesh['rep'=2,'ep'=8,'tp'=2] {'tp'}, use_global_device_ids=true, to_apply=%region_11.12 | all-reduce | flops 64 | bytes 512 | tf_op jit(solution)/shard_map/psum | solution.py:54
  75.9 0.5 convolution_convert_fusion
  76.4 0.3 copy.59
  76.7 26.2 %all_to_all.10 = bf16[8,1,64,720]{3,2,1,0:T(8,128)(2,1)S(1)} all-to-all(bf16[8,1,64,720]{3,2,1,0:T(8,128)(2,1)S(1)} %bitcast.116), channel_id=1, replica_groups=mesh['rep'=2,'ep'=8,'tp'=2] {'ep'}, dimensions={0} | all-to-all | bytes 1474560 | tf_op jit(solution)/shard_map/all_to_all | solution.py:80
  102.9 1.8 copy.61
  104.7 0.0 all-gather.2.cloned.1.call-update
  104.7 0.0 reduce-scatter.9.cloned.1.call-start
  104.8 11.0 %all-gather.2.cloned.1.call-done = bf16[8,1,64,1440]{2,0,1,3:T(8,128)(2,1)} async-done(((bf16[8,1,64,720]{2,0,1,3:T(8,128)(2,1)}), bf16[8,1,64,1440]{2,0,1,3:T(8,128)(2,1)}) %all-gather.2.cloned.1.call-update) | async-done | bytes 1474576 | tf_op jit(solution)/shard_map/all_gather | solution.py:79
  115.7 3.7 %copy.62 = bf16[8,1,64,1440]{3,2,0,1:T(8,128)(2,1)S(1)} copy(bf16[8,1,64,1440]{2,0,1,3:T(8,128)(2,1)} %all-gather.2.cloned.1.call-done) | data formatting | bytes 2949120 | tf_op jit(solution)/shard_map/all_gather | solution.py:79
  119.4 4.2 %fusion.8 = f32[8,64,720]{2,1,0:T(8,128)} fusion(bf16[1,1440,720]{2,1,0:T(8,128)(2,1)} %param.21, bf16[8,1,64,1440]{3,2,0,1:T(8,128)(2,1)S(1)} %copy.62), kind=kOutput, calls=%fused_computation.14 | convolution fusion | flops 1061683200 | bytes 5022720 | tf_op jit(solution)/shard_map/sekd,edf->sekf/dot_general | solution.py:85
  123.6 7.7 %convolution_bitcast_fusion = f32[8,1,64,1440]{3,2,0,1:T(8,128)} fusion(bf16[1,720,1440]{2,1,0:T(8,128)(2,1)} %param.23, bf16[1,1440,720]{2,1,0:T(8,128)(2,1)} %param.22, bf16[8,1,64,1440]{3,2,0,1:T(8,128)(2,1)S(1)} %copy.62, f32[8,64,720]{2,1,0:T(8,128)} %fusion.8), kind=kOutput, calls=%fused_computation.7 | convolution fusion | flops 2126315520 | bytes 10045440 | tf_op jit(solution)/shard_map/sekf,efd->sekd/dot_general | solution.py:92
  131.2 5.7 %copy.66 = f32[8,1,64,1440]{2,0,1,3:T(8,128)} copy(f32[8,1,64,1440]{3,2,0,1:T(8,128)} %convolution_bitcast_fusion) | data formatting | bytes 5898240
  137.0 5.9 %reshape.126 = f32[1440,512]{1,0:T(8,128)} reshape(f32[1440,1,8,64]{3,2,1,0:T(8,128)} %bitcast.113) | data formatting | bytes 5898240
  142.8 0.0 reduce-scatter.9.cloned.1.call-update
  142.9 12.2 %reduce-scatter.9.cloned.1.call-done = f32[720,512]{1,0:T(8,128)} async-done(((f32[1440,512]{1,0:T(8,128)}), f32[720,512]{1,0:T(8,128)}) %reduce-scatter.9.cloned.1.call-update) | async-done | bytes 1474576
  155.1 3.1 %reshape.127 = bf16[720,1,8,64]{3,2,1,0:T(8,128)(2,1)} reshape(f32[720,512]{1,0:T(8,128)} %reduce-scatter.9.cloned.1.call-done) | data formatting | bytes 2211840
  158.2 2.9 %copy.67 = bf16[8,1,64,720]{3,2,0,1:T(8,128)(2,1)} copy(bf16[8,1,64,720]{2,0,1,3:T(8,128)(2,1)} %bitcast.114) | data formatting | bytes 1474560
  161.1 26.3 %all_to_all.11 = bf16[8,1,64,720]{3,2,1,0:T(8,128)(2,1)S(1)} all-to-all(bf16[8,1,64,720]{3,2,1,0:T(8,128)(2,1)} %bitcast.117), channel_id=1, replica_groups=mesh['rep'=2,'ep'=8,'tp'=2] {'ep'}, dimensions={0} | all-to-all | bytes 1474560 | tf_op jit(solution)/shard_map/all_to_all | solution.py:96
  187.4 1.2 fusion.40
  188.6 0.0 copy-done.1
  (12 shorter events, 0.1 us)
Async XLA Ops:
  6.5 52.7 %copy-start = (bf16[1024,1440]{0,1:T(8,128)(2,1)S(1)}, bf16[1024,1440]{0,1:T(8,128)(2,1)}, u32[]{:S(2)}) copy-start(bf16[1024,1440]{0,1:T(8,128)(2,1)} %param.20) | copy-start | bytes 8847364
  6.5 6.7 %copy-start.6 = (s32[64,12]{0,1:T(8,128)S(1)}, s32[64,12]{0,1:T(8,128)}, u32[]{:S(2)}) copy-start(s32[64,12]{0,1:T(8,128)} %param.15) | copy-start | bytes 9220
  6.5 65.6 %reduce-scatter.7.cloned.1.call-start = ((), (), s32[]{:S(2)}) async-start(), calls=%async_computation.5 | async-start | bytes 1105920
  18.3 11.7 %copy-start.3 = (bf16[64,1024]{1,0:T(8,128)(2,1)S(1)}, bf16[64,1024]{1,0:T(8,128)(2,1)}, u32[]{:S(2)}) copy-start(bf16[64,1024]{1,0:T(8,128)(2,1)} %param.13) | copy-start | bytes 393220
  18.3 11.8 %copy-start.8 = (s32[64]{0:T(128)S(1)}, s32[64]{0:T(128)}, u32[]{:S(2)}) copy-start(s32[64]{0:T(128)} %param.16) | copy-start | bytes 772
  59.2 2.1 %copy-start.5 = (s32[64,4]{0,1:T(4,128)S(1)}, s32[64,4]{0,1:T(4,128)}, u32[]{:S(2)}) copy-start(s32[64,4]{0,1:T(4,128)} %param.17) | copy-start | bytes 3076
  59.2 3.5 %copy-start.7 = (f32[1440]{0:T(1024)S(1)}, f32[1440]{0:T(1024)}, u32[]{:S(2)}) copy-start(f32[1440]{0:T(1024)} %param.19) | copy-start | bytes 17284
  59.3 3.6 %copy-start.4 = (f32[64,4]{0,1:T(4,128)S(1)}, f32[64,4]{0,1:T(4,128)}, u32[]{:S(2)}) copy-start(f32[64,4]{0,1:T(4,128)} %param.18) | copy-start | bytes 3076
  59.3 14.0 %copy-start.2 = (bf16[64,1440]{1,0:T(8,128)(2,1)S(1)}, bf16[64,1440]{1,0:T(8,128)(2,1)}, u32[]{:S(2)}) copy-start(bf16[64,1440]{1,0:T(8,128)(2,1)} %param.12) | copy-start | bytes 552964
  61.1 54.6 %all-gather.2.cloned.1.call-start = ((), (), s32[]{:S(2)}) async-start(), calls=%async_computation.4 | async-start | bytes 4423680 | tf_op jit(solution)/shard_map/all_gather | solution.py:79
  104.7 50.4 %reduce-scatter.9.cloned.1.call-start = ((), (), s32[]{:S(2)}) async-start(), calls=%async_computation.6 | async-start | bytes 4423680
  158.2 30.4 %copy-start.1 = (bf16[1024,1440]{0,1:T(8,128)(2,1)S(1)}, bf16[1024,1440]{0,1:T(8,128)(2,1)}, u32[]{:S(2)}) copy-start(bf16[1024,1440]{0,1:T(8,128)(2,1)} %param.20) | copy-start | bytes 8847364
Sparse Core Ops, SparseCore 0:
  61.2 10.8 reduce-scatter.6
  104.9 10.8 all-gather.1
  143.0 12.0 reduce-scatter.8
where the time goes:
time: 196 us; the launch traced here: 195 us
  local copies, waits for them, and re-layouts  65.6 us (33%)
  blocking collectives  54.9 us (28%)
  waiting for transfers between devices  32.2 us (16%)
  matrix products  27.5 us (14%)
  between operations  13.3 us (7%)
    all_to_all x1, blocking collectives, body(): lax.all_to_all(finished, 'ep', split_axis=0, concat_axis=0, tiled=True)  26.3 us
    all_to_all x1, blocking collectives, body(): lax.all_to_all(outgoing, 'ep', split_axis=0, concat_axis=0, tiled=True)  26.2 us
    unnamed x5, waiting for transfers between devices  21.3 us
    unnamed x24, local copies, waits for them, and re-layouts  18.9 us
    reshape x1, local copies, waits for them, and re-layouts, body(): key_value_pages[0][page_table]  11.7 us
    reshape x1, local copies, waits for them, and re-layouts, body(): key_value_pages[1][page_table]  11.6 us
    all_gather x1, waiting for transfers between devices, body(): lax.all_gather(lax.all_to_all(outgoing, 'ep', split_axis=0, concat_axis=0...  11 us
    dot_general x1, matrix products, body(): jnp.einsum('sekf,efd->sekd', hidden, w_down, preferred_element_type=jnp.f...  7.66 us
  transfers between devices with their start and end apart: 3, of which 3 were waited for; matrix products, arithmetic and copies ran while one was open for 1% of the time, Pallas kernels for 0%

commit v1 on v0

--- a/solution.py
+++ b/solution.py
@@ -3,6 +3,7 @@
 import jax.numpy as jnp
 from jax import lax
 from jax.sharding import PartitionSpec as P
+from jax.lax import all_to_all, axis_size
 
 HEAD_WIDTH = 64
 
@@ -21,6 +22,11 @@
     w_up,
     w_down,
 ):
+
+    def review_the_works(xs):
+        top = jnp.stack([xs] * axis_size("tp"), axis=0)
+        return jnp.concatenate(all_to_all(top, "tp", 0, 0), axis=3)
+
     tok_rows = query.shape[0]
     model_width = resid.shape[1]
     query_heads = query.shape[1] // HEAD_WIDTH
@@ -76,11 +82,8 @@
     outgoing = outgoing.astype(jnp.bfloat16).reshape(
         owners, local_experts, capacity, normed.shape[1]
     )
-    arrived_full = lax.all_gather(
-        lax.all_to_all(outgoing, "ep", split_axis=0, concat_axis=0, tiled=True),
-        "tp",
-        axis=3,
-        tiled=True,
+    arrived_full = review_the_works(
+        lax.all_to_all(outgoing, "ep", split_axis=0, concat_axis=0, tiled=True)
     )
     gate_value = jnp.einsum(
         "sekd,edf->sekf", arrived_full, w_gate, preferred_element_type=jnp.float32

time: 196 us -> 187 us (0.954)
  waiting for transfers between devices: 32.2 us -> 19.1 us
  blocking collectives: 54.9 us -> 59.9 us
    all_gather x1 -> x0, waiting for transfers between devices: 11 us -> none  [body(): lax.all_gather(lax.all_to_all(outgoing, 'ep', split_axis=0, concat_axis=0...]
    all_to_all x0 -> x1, blocking collectives: none -> 5 us  [review_the_works(): return jnp.concatenate(all_to_all(top, 'tp', 0, 0), axis=3)]
    all_gather x1 -> x0, local copies, waits for them, and re-layouts: 3.66 us -> none  [body(): lax.all_gather(lax.all_to_all(outgoing, 'ep', split_axis=0, concat_axis=0...]
    unnamed x5 -> x4, waiting for transfers between devices: 21.3 us -> 19.1 us
    another operation x1 -> x2, local copies, waits for them, and re-layouts: 0.01 us -> 2.11 us
    unnamed x24 -> x26, local copies, waits for them, and re-layouts: 18.9 us -> 18.9 us
  transfers between devices with their start and end apart: 3 -> 2, of which waited for: 3 -> 2; matrix products, arithmetic and copies ran while one was open for 1% -> 1% of each run, Pallas kernels for 0% -> 0%
where the time goes in v1:
time: 187 us; the launch traced here: 186 us
  local copies, waits for them, and re-layouts  63.9 us (34%)
  blocking collectives  59.9 us (32%)
  matrix products  28.1 us (15%)
  waiting for transfers between devices  19.1 us (10%)
  between operations  13.6 us (7%)
    all_to_all x1, blocking collectives, body(): lax.all_to_all(finished, 'ep', split_axis=0, concat_axis=0, tiled=True)  26.3 us
    all_to_all x1, blocking collectives, body(): lax.all_to_all(outgoing, 'ep', split_axis=0, concat_axis=0, tiled=True)  26.2 us
    unnamed x4, waiting for transfers between devices  19.1 us
    unnamed x26, local copies, waits for them, and re-layouts  18.9 us
    reshape x1, local copies, waits for them, and re-layouts, body(): key_value_pages[0][page_table]  11.7 us
    reshape x1, local copies, waits for them, and re-layouts, body(): key_value_pages[1][page_table]  11.6 us
    dot_general x1, matrix products, body(): jnp.einsum('sekf,efd->sekd', hidden, w_down, preferred_element_type=jnp.f...  7.66 us
    sub x1, matrix products, body(): weights = jnp.exp(scores - row_max)  7.32 us
  transfers between devices with their start and end apart: 2, of which 2 were waited for; matrix products, arithmetic and copies ran while one was open for 1% of the time, Pallas kernels for 0%

profile of v1, /device:TPU:0, one launch (start us, length us, event | category | flops | bytes accessed | tf_op | source)
XLA Modules:
  0.0 186.2 jit_solution(17113803546833560919)
XLA Ops:
  6.5 0.0 copy-start
  6.5 0.0 copy-start.7
  6.5 0.0 reduce-scatter.7.cloned.1.call-start
  6.5 6.7 %slice_bitcast_fusion.1 = (bf16[768,16,128]{2,1,0:T(8,128)(2,1)}, bf16[768,16,128]{2,1,0:T(8,128)(2,1)}) fusion(bf16[2,768,16,128]{3,2,1,0:T(8,128)(2,1)} %param.14), kind=kLoop, calls=%fused_computation.9 | loop fusion | bytes 12582912 | tf_op jit(solution)/shard_map/squeeze | solution.py:36
  13.3 0.0 copy-done.7
  13.3 0.1 copy.52
  13.4 0.1 reshape.108
  13.5 4.9 %gather_fusion = bf16[768,16,128]{2,1,0:T(8,128)(2,1)} fusion(bf16[768,16,128]{2,1,0:T(8,128)(2,1)} %get-tuple-element.7, s32[1024]{0:T(1024)S(1)} %pad_clamp_fusion), kind=kCustom, calls=%fused_computation | custom fusion | bytes 6294528 | tf_op jit(solution)/shard_map/gather | solution.py:36
  18.3 0.0 copy-start.4
  18.3 11.7 %reshape.93 = bf16[64,192,2,64]{3,2,1,0:T(2,128)(2,1)} reshape(bf16[768,16,128]{2,1,0:T(8,128)(2,1)} %gather_fusion) | data formatting | bytes 6291456 | tf_op jit(solution)/shard_map/reshape | solution.py:36
  30.0 0.0 copy-done.4
  30.0 0.2 reshape.94
  30.2 0.0 copy-done.9
  30.2 0.1 iota_compare_fusion.1
  30.3 4.9 %gather_fusion.1 = bf16[768,16,128]{2,1,0:T(8,128)(2,1)} fusion(bf16[768,16,128]{2,1,0:T(8,128)(2,1)} %get-tuple-element.8, s32[1024]{0:T(1024)S(1)} %pad_clamp_fusion), kind=kCustom, calls=%fused_computation.1 | custom fusion | bytes 6294528 | tf_op jit(solution)/shard_map/gather | solution.py:39
  35.2 11.6 %reshape.95 = bf16[64,192,2,64]{3,2,1,0:T(2,128)(2,1)} reshape(bf16[768,16,128]{2,1,0:T(8,128)(2,1)} %gather_fusion.1) | data formatting | bytes 6291456 | tf_op jit(solution)/shard_map/reshape | solution.py:39
  46.8 7.3 %fusion.52 = (f32[64,2,8]{2,1,0:T(2,128)S(1)}, f32[64,2,8,192]{3,2,1,0:T(8,128)}) fusion(bf16[64,2,8,64]{3,2,1,0:T(8,128)(2,1)S(1)} %reshape.94, bf16[64,192,2,64]{3,2,1,0:T(2,128)(2,1)} %reshape.93, pred[64,192]{1,0:T(8,128)(4,1)S(1)} %iota_compare_fusion.1), kind=kOutput, calls=%fused_computation.68 | convolution fusion | flops 25952448 | bytes 4079616 | tf_op jit(solution)/shard_map/sub | solution.py:49
  54.1 4.9 %fusion.31 = bf16[64,2,8,64]{3,2,1,0:T(8,128)(2,1)S(1)} fusion(bf16[64,192,2,64]{3,2,1,0:T(2,128)(2,1)} %reshape.95, f32[64,2,8,192]{3,2,1,0:T(8,128)} %get-tuple-element.10, f32[64,2,8]{2,1,0:T(2,128)S(1)} %get-tuple-element.9), kind=kOutput, calls=%fused_computation.32 | convolution fusion | flops 25624576 | bytes 4067328 | tf_op jit(solution)/shard_map/tgqp,tpgd->tgqd/dot_general | solution.py:51
  59.0 0.2 reshape.96
  59.2 0.0 copy-done
  59.2 0.0 copy-start.6
  59.2 0.0 copy-start.8
  59.3 0.0 copy-start.5
  59.3 0.0 copy-start.3
  59.3 1.8 convolution_bitcast_fusion.1
  61.1 0.0 reduce-scatter.7.cloned.1.call-update
  61.1 0.2 reduce-scatter.9.cloned.1.call-start
  61.3 0.0 copy-done.6
  61.3 0.1 copy.55
  61.4 0.1 eq.42
  61.5 0.1 eq.38
  61.7 0.6 reduce-window.6
  62.2 0.2 slice_reduce_fusion
  62.5 0.1 fusion.45
  62.6 0.1 reduce_sum.58
  62.7 0.1 copy.57
  62.8 0.0 copy-done.8
  62.8 0.1 dynamic_slice.7
  62.9 0.0 copy-done.5
  62.9 0.2 convert_reduce_fusion
  63.1 9.0 %reduce-scatter.7.cloned.1.call-done = f32[720,64]{1,0:T(8,128)} async-done(((f32[1440,64]{1,0:T(8,128)}), f32[720,64]{1,0:T(8,128)}) %reduce-scatter.7.cloned.1.call-update) | async-done | bytes 184336
  72.1 1.1 copy.63
  73.2 0.0 copy-done.3
  73.3 0.2 multiply_reduce_fusion
  73.5 2.5 %psum.7 = f32[64]{0:T(128)S(1)} all-reduce(f32[64]{0:T(128)S(1)} %multiply_reduce_fusion), channel_id=1, replica_groups=mesh['rep'=2,'ep'=8,'tp'=2] {'tp'}, use_global_device_ids=true, to_apply=%region_11.12 | all-reduce | flops 64 | bytes 512 | tf_op jit(solution)/shard_map/psum | solution.py:60
  75.9 0.5 convolution_convert_fusion
  76.4 0.3 copy.58
  76.7 26.2 %all_to_all.15 = bf16[8,1,64,720]{3,2,1,0:T(8,128)(2,1)S(1)} all-to-all(bf16[8,1,64,720]{3,2,1,0:T(8,128)(2,1)S(1)} %bitcast.112), channel_id=1, replica_groups=mesh['rep'=2,'ep'=8,'tp'=2] {'ep'}, dimensions={0} | all-to-all | bytes 1474560 | tf_op jit(solution)/shard_map/all_to_all | solution.py:86
  102.9 0.2 pad_maximum_fusion
  103.0 5.0 %all_to_all.16 = bf16[2,8,1,64,720]{4,3,1,2,0:T(8,128)(2,1)S(1)} all-to-all(bf16[2,8,1,64,720]{4,3,1,2,0:T(8,128)(2,1)S(1)} %pad_maximum_fusion), channel_id=1, replica_groups=mesh['rep'=2,'ep'=8,'tp'=2] {'tp'}, dimensions={0} | all-to-all | bytes 2949120 | tf_op jit(solution)/shard_map/all_to_all | solution.py:28
  108.0 1.6 copy.60
  109.7 2.1 %reshape.100 = bf16[8,64,1440]{2,1,0:T(8,128)(2,1)} reshape(bf16[8,1,64,2,720]{4,3,2,0,1:T(2,128)(2,1)S(1)} %copy.60) | data formatting | bytes 2949120 | tf_op jit(solution)/shard_map/reshape.4
  111.8 4.8 %fusion.8 = f32[8,64,720]{2,1,0:T(8,128)} fusion(bf16[8,64,1440]{2,1,0:T(8,128)(2,1)} %reshape.100, bf16[1,1440,720]{2,1,0:T(8,128)(2,1)} %param.21), kind=kOutput, calls=%fused_computation.14 | convolution fusion | flops 1061683200 | bytes 5022720 | tf_op jit(solution)/shard_map/sekd,edf->sekf/dot_general | solution.py:88
  116.5 0.0 copy-done.2
  116.5 7.7 %convolution_bitcast_fusion = f32[8,1,64,1440]{3,2,0,1:T(8,128)} fusion(bf16[1,720,1440]{2,1,0:T(8,128)(2,1)} %param.23, bf16[8,64,1440]{2,1,0:T(8,128)(2,1)S(1)} %copy-done.2, bf16[1,1440,720]{2,1,0:T(8,128)(2,1)} %param.22, f32[8,64,720]{2,1,0:T(8,128)} %fusion.8), kind=kOutput, calls=%fused_computation.7 | convolution fusion | flops 2126315520 | bytes 10045440 | tf_op jit(solution)/shard_map/sekf,efd->sekd/dot_general | solution.py:95
  124.2 5.7 %copy.64 = f32[8,1,64,1440]{2,0,1,3:T(8,128)} copy(f32[8,1,64,1440]{3,2,0,1:T(8,128)} %convolution_bitcast_fusion) | data formatting | bytes 5898240
  129.9 5.9 %reshape.133 = f32[1440,512]{1,0:T(8,128)} reshape(f32[1440,1,8,64]{3,2,1,0:T(8,128)} %bitcast.108) | data formatting | bytes 5898240
  135.8 0.0 reduce-scatter.9.cloned.1.call-update
  135.8 10.1 %reduce-scatter.9.cloned.1.call-done = f32[720,512]{1,0:T(8,128)} async-done(((f32[1440,512]{1,0:T(8,128)}), f32[720,512]{1,0:T(8,128)}) %reduce-scatter.9.cloned.1.call-update) | async-done | bytes 1474576
  145.9 3.1 %reshape.134 = bf16[720,1,8,64]{3,2,1,0:T(8,128)(2,1)} reshape(f32[720,512]{1,0:T(8,128)} %reduce-scatter.9.cloned.1.call-done) | data formatting | bytes 2211840
  149.0 2.9 %copy.65 = bf16[8,1,64,720]{3,2,0,1:T(8,128)(2,1)} copy(bf16[8,1,64,720]{2,0,1,3:T(8,128)(2,1)} %bitcast.110) | data formatting | bytes 1474560
  151.9 26.3 %all_to_all.17 = bf16[8,1,64,720]{3,2,1,0:T(8,128)(2,1)S(1)} all-to-all(bf16[8,1,64,720]{3,2,1,0:T(8,128)(2,1)} %bitcast.113), channel_id=1, replica_groups=mesh['rep'=2,'ep'=8,'tp'=2] {'ep'}, dimensions={0} | all-to-all | bytes 1474560 | tf_op jit(solution)/shard_map/all_to_all | solution.py:99
  178.2 1.2 fusion.34
  179.3 0.0 copy-done.1
  (13 shorter events, 0.1 us)
Async XLA Ops:
  6.5 52.7 %copy-start = (bf16[1024,1440]{0,1:T(8,128)(2,1)S(1)}, bf16[1024,1440]{0,1:T(8,128)(2,1)}, u32[]{:S(2)}) copy-start(bf16[1024,1440]{0,1:T(8,128)(2,1)} %param.20) | copy-start | bytes 8847364
  6.5 6.7 %copy-start.7 = (s32[64,12]{0,1:T(8,128)S(1)}, s32[64,12]{0,1:T(8,128)}, u32[]{:S(2)}) copy-start(s32[64,12]{0,1:T(8,128)} %param.15) | copy-start | bytes 9220
  6.5 65.6 %reduce-scatter.7.cloned.1.call-start = ((), (), s32[]{:S(2)}) async-start(), calls=%async_computation.5 | async-start | bytes 1105920
  18.3 11.7 %copy-start.4 = (bf16[64,1024]{1,0:T(8,128)(2,1)S(1)}, bf16[64,1024]{1,0:T(8,128)(2,1)}, u32[]{:S(2)}) copy-start(bf16[64,1024]{1,0:T(8,128)(2,1)} %param.13) | copy-start | bytes 393220
  18.3 11.8 %copy-start.9 = (s32[64]{0:T(128)S(1)}, s32[64]{0:T(128)}, u32[]{:S(2)}) copy-start(s32[64]{0:T(128)} %param.16) | copy-start | bytes 772
  59.2 2.1 %copy-start.6 = (s32[64,4]{0,1:T(4,128)S(1)}, s32[64,4]{0,1:T(4,128)}, u32[]{:S(2)}) copy-start(s32[64,4]{0,1:T(4,128)} %param.17) | copy-start | bytes 3076
  59.2 3.5 %copy-start.8 = (f32[1440]{0:T(1024)S(1)}, f32[1440]{0:T(1024)}, u32[]{:S(2)}) copy-start(f32[1440]{0:T(1024)} %param.19) | copy-start | bytes 17284
  59.3 3.6 %copy-start.5 = (f32[64,4]{0,1:T(4,128)S(1)}, f32[64,4]{0,1:T(4,128)}, u32[]{:S(2)}) copy-start(f32[64,4]{0,1:T(4,128)} %param.18) | copy-start | bytes 3076
  59.3 14.0 %copy-start.3 = (bf16[64,1440]{1,0:T(8,128)(2,1)S(1)}, bf16[64,1440]{1,0:T(8,128)(2,1)}, u32[]{:S(2)}) copy-start(bf16[64,1440]{1,0:T(8,128)(2,1)} %param.12) | copy-start | bytes 552964
  61.1 84.8 %reduce-scatter.9.cloned.1.call-start = ((), (), s32[]{:S(2)}) async-start(), calls=%async_computation.6 | async-start | bytes 4423680
  111.8 4.8 %copy-start.2 = (bf16[8,64,1440]{2,1,0:T(8,128)(2,1)S(1)}, bf16[8,64,1440]{2,1,0:T(8,128)(2,1)}, u32[]{:S(2)}) copy-start(bf16[8,64,1440]{2,1,0:T(8,128)(2,1)} %reshape.100) | copy-start | bytes 4423684
  149.0 30.4 %copy-start.1 = (bf16[1024,1440]{0,1:T(8,128)(2,1)S(1)}, bf16[1024,1440]{0,1:T(8,128)(2,1)}, u32[]{:S(2)}) copy-start(bf16[1024,1440]{0,1:T(8,128)(2,1)} %param.20) | copy-start | bytes 8847364
Sparse Core Ops, SparseCore 0:
  61.2 10.8 reduce-scatter.6
  135.9 9.9 reduce-scatter.8
